TPU v7x, 32 devices: a whole 2x2x4 slice. The times are simulated.
32 devices in a mesh: inter: 16 (over z, y, x), intra: 2 (over core).
Axes of the slice: x: 2, y: 2, z: 4, core: 2. Of those that a mesh axis runs over, the one named last changes fastest.
Arguments:
- tokens: bfloat16 [2048, 4096], P('inter', 'intra'), may hold values from -6 to 6
- gate_codes: bfloat16 [7168, 4096], P(('intra', 'inter')), may hold values from -127 to 127
- gate_scales: float32 [7168, 16], P(('intra', 'inter')), may hold values from 0.0001 to 0.0005
- up_codes: bfloat16 [7168, 4096], P(('intra', 'inter')), may hold values from -127 to 127
- up_scales: float32 [7168, 16], P(('intra', 'inter')), may hold values from 0.0001 to 0.0005
- cotangent: bfloat16 [2048, 7168], P('inter', 'intra'), may hold values from -6 to 6
Outputs:
- hidden: bfloat16 [2048, 7168], P('inter', 'intra')
- token_grad: bfloat16 [2048, 4096], P('inter', 'intra')
- gate_grad: float32 [7168, 4096], P(('intra', 'inter'))
- up_grad: float32 [7168, 4096], P(('intra', 'inter'))
All inputs are finite; a program needn't handle non-finite values.
Results may differ from a plain program's by a relative error of at most 0.02.
Values may be sent and summed in bfloat16 or wider, within the bound.
A program may use at most 384 MiB of HBM per device.

v0:
```python
import jax
import jax.numpy as jnp
from jax import lax
from jax.sharding import PartitionSpec as P


def dequantize(codes, scales):
    rows, width = codes.shape
    blocks = scales.shape[1]
    step = width // blocks
    parts = [
        codes[:, b * step : (b + 1) * step].astype(jnp.float32) * scales[:, b : b + 1]
        for b in range(blocks)
    ]
    return jnp.concatenate(parts, axis=1).astype(jnp.bfloat16)


def per_device(tokens, gate_codes, gate_scales, up_codes, up_scales, cotangent):
    groups = lax.axis_size("inter")
    mine = lax.all_gather(tokens, "inter", axis=0, tiled=True)
    whole = lax.all_gather(mine, "intra", axis=0, tiled=False)
    slabs, count, wide = whole.shape
    back = lax.all_to_all(cotangent, "inter", split_axis=1, concat_axis=0, tiled=True)
    w_gate = dequantize(gate_codes, gate_scales)
    w_up = dequantize(up_codes, up_scales)

    def forward(weights):
        total = None
        for s in range(slabs):
            term = lax.dot_general(
                whole[s],
                weights[:, s * wide : (s + 1) * wide],
                (((1,), (1,)), ((), ())),
                preferred_element_type=jnp.float32,
            )
            total = term if total is None else total + term
        return total

    gate = forward(w_gate)
    up = forward(w_up)
    sig = jax.nn.sigmoid(gate)
    act = gate * sig
    hidden = (act * up).astype(jnp.bfloat16)
    back = back.astype(jnp.float32)
    d_up = (back * act).astype(jnp.bfloat16)
    d_gate = (back * up * sig * (1.0 + gate * (1.0 - sig))).astype(jnp.bfloat16)
    hidden = lax.all_to_all(hidden, "inter", split_axis=0, concat_axis=1, tiled=True)
    partial_sum = jnp.dot(d_gate, w_gate, preferred_element_type=jnp.float32)
    partial_sum = partial_sum + jnp.dot(d_up, w_up, preferred_element_type=jnp.float32)
    partial_sum = lax.psum_scatter(
        partial_sum.astype(jnp.bfloat16), "intra", scatter_dimension=1, tiled=True
    )
    token_grad = lax.psum_scatter(partial_sum, "inter", scatter_dimension=0, tiled=True)

    def rows_grad(d_rows):
        terms = [
            lax.dot_general(
                d_rows, whole[s], (((0,), (0,)), ((), ())), preferred_element_type=jnp.float32
            )
            for s in range(slabs)
        ]
        return jnp.concatenate(terms, axis=1) / groups

    return (hidden, token_grad, rows_grad(d_gate), rows_grad(d_up))


def solution(mesh):
    return jax.shard_map(
        per_device,
        mesh=mesh,
        in_specs=(
            P("inter", "intra"),
            P(("intra", "inter"), None),
            P(("intra", "inter"), None),
            P(("intra", "inter"), None),
            P(("intra", "inter"), None),
            P("inter", "intra"),
        ),
        out_specs=(
            P("inter", "intra"),
            P("inter", "intra"),
            P(("intra", "inter"), None),
            P(("intra", "inter"), None),
        ),
        check_vma=False,
    )
```

profile of v0, /device:TPU:26, one launch (start us, length us, event | category | flops | bytes accessed | tf_op | source)
XLA Modules:
  0.0 465.3 jit_solution(1570176110932852104)
XLA Ops:
  7.9 114.0 %all-gather.4.cloned.1.call-done = bf16[2048,2048]{1,0:T(8,128)(2,1)} async-done(((bf16[128,2048]{1,0:T(8,128)(2,1)}), bf16[2048,2048]{1,0:T(8,128)(2,1)}) %all-gather.4.cloned.1.call-update) | async-done | bytes 8388624 | tf_op jit(solution)/shard_map/all_gather | solution.py:20
  124.4 6.3 %all-to-all-start.1 = ((bf16[128,16,224]{0,2,1:T(8,128)(2,1)}), bf16[128,16,224]{0,2,1:T(8,128)(2,1)S(1)}, u32[]{:S(2)}, u32[]{:S(2)}) async-start(bf16[128,16,224]{0,2,1:T(8,128)(2,1)} %bitcast.36), calls=%async_computation.1 | async-start | bytes 1835008 | tf_op jit(solution)/shard_map/all_to_all | solution.py:23
  141.2 1.7 constant_dynamic-update-slice_fusion.47
  143.0 1.7 constant_dynamic-update-slice_fusion.46
  144.7 1.7 constant_dynamic-update-slice_fusion.45
  146.3 1.6 constant_dynamic-update-slice_fusion.44
  148.0 1.6 constant_dynamic-update-slice_fusion.43
  151.3 1.6 constant_dynamic-update-slice_fusion.41
  152.9 1.6 constant_dynamic-update-slice_fusion.40
  154.6 1.8 constant_dynamic-update-slice_fusion.39
  164.3 1.7 constant_dynamic-update-slice_fusion.38
  166.0 1.7 constant_dynamic-update-slice_fusion.37
  167.7 1.7 constant_dynamic-update-slice_fusion.36
  169.4 1.7 constant_dynamic-update-slice_fusion.35
  171.0 1.7 constant_dynamic-update-slice_fusion.34
  172.7 1.7 constant_dynamic-update-slice_fusion.33
  174.4 1.7 constant_dynamic-update-slice_fusion.32
  176.1 7.7 %fusion.2 = f32[224,2048]{1,0:T(8,128)} fusion(bf16[224,2048]{1,0:T(8,128)(2,1)} %copy-done.7, bf16[4096,2048]{1,0:T(8,128)(2,1)} %all-gather.6.cloned.1.call-done), kind=kOutput, calls=%fused_computation.3 | convolution fusion | flops 1879048192 | bytes 11141120 | tf_op jit(solution)/shard_map/dot_general | solution.py:30
  183.8 6.7 %fusion.4 = f32[224,2048]{1,0:T(8,128)S(1)} fusion(bf16[224,2048]{1,0:T(8,128)(2,1)} %get-tuple-element.44, bf16[4096,2048]{1,0:T(8,128)(2,1)} %all-gather.6.cloned.1.call-done), kind=kOutput, calls=%fused_computation.5 | convolution fusion | flops 1879048192 | bytes 11141120 | tf_op jit(solution)/shard_map/dot_general | solution.py:30
  190.5 3.9 fusion.19
  195.3 9.3 %fusion.31 = (bf16[2048,224]{0,1:T(8,128)(2,1)S(1)}, bf16[2048,224]{0,1:T(8,128)(2,1)S(1)}, bf16[28,16,8,128]{3,2,1,0:T(8,128)(2,1)}) fusion(f32[2048,224]{0,1:T(8,128)} %fusion.19, f32[224,2048]{1,0:T(8,128)} %fusion.2, bf16[224,2048]{1,0:T(8,128)(2,1)} %copy-done.8, bf16[4096,2048]{1,0:T(8,128)(2,1)} %all-gather.6.cloned.1.call-done, ...), kind=kOutput, calls=%fused_computation.28 | convolution fusion | flops 1886846976 | bytes 16646144 | tf_op jit(solution)/shard_map/dot_general | solution.py:30
  204.6 15.0 %fusion.38 = f32[2048,4096]{1,0:T(8,128)} fusion(bf16[2048,224]{0,1:T(8,128)(2,1)S(1)} %get-tuple-element.9, bf16[224,4096]{1,0:T(8,128)(2,1)} %get-tuple-element.43), kind=kOutput, calls=%fused_computation.133 | convolution fusion | flops 3758096384 | bytes 36306944 | tf_op jit(solution)/shard_map/dot_general | solution.py:48
  219.6 16.9 %add_convert_fusion = bf16[2048,4096]{1,0:T(8,128)(2,1)} fusion(f32[2048,4096]{1,0:T(8,128)} %fusion.38, bf16[2048,224]{0,1:T(8,128)(2,1)S(1)} %get-tuple-element.8, bf16[224,4096]{1,0:T(8,128)(2,1)S(1)} %get-tuple-element.11), kind=kOutput, calls=%fused_computation | convolution fusion | flops 3774873600 | bytes 53084160 | tf_op jit(solution)/shard_map/dot_general | solution.py:49
  236.6 26.3 %reduce-scatter.3.cloned.1.call-done = bf16[2048,2048]{1,0:T(8,128)(2,1)} async-done(((bf16[2048,4096]{1,0:T(8,128)(2,1)}), bf16[2048,2048]{1,0:T(8,128)(2,1)}) %reduce-scatter.3.cloned.1.call-update) | async-done | bytes 8388624 | tf_op jit(solution)/shard_map/reduce_scatter | solution.py:50
  265.1 6.9 %all-to-all-start = ((bf16[16,128,224]{1,2,0:T(8,128)(2,1)}), bf16[16,128,224]{1,2,0:T(8,128)(2,1)S(1)}, u32[]{:S(2)}, u32[]{:S(2)}) async-start(bf16[16,128,224]{1,2,0:T(8,128)(2,1)} %bitcast.73), calls=%async_computation | async-start | bytes 1835008 | tf_op jit(solution)/shard_map/all_to_all | solution.py:47
  272.1 5.9 %fusion.6 = f32[224,2048]{1,0:T(8,128)S(1)} fusion(bf16[2048,224]{0,1:T(8,128)(2,1)S(1)} %copy-done.4, bf16[4096,2048]{1,0:T(8,128)(2,1)} %all-gather.6.cloned.1.call-done), kind=kOutput, calls=%fused_computation.7 | convolution fusion | flops 1879048192 | bytes 11141120 | tf_op jit(solution)/shard_map/dot_general | solution.py:57
  278.0 5.6 %fusion.14 = f32[224,2048]{1,0:T(8,128)S(1)} fusion(bf16[2048,224]{0,1:T(8,128)(2,1)S(1)} %copy-done.4, bf16[4096,2048]{1,0:T(8,128)(2,1)} %all-gather.6.cloned.1.call-done), kind=kOutput, calls=%fused_computation.15 | convolution fusion | flops 1879048192 | bytes 11141120 | tf_op jit(solution)/shard_map/dot_general | solution.py:57
  283.8 2.1 fusion
  285.9 2.1 fusion.8
  288.1 3.5 maximum_multiply_fusion
  291.6 14.6 %all-to-all-done = bf16[16,128,224]{1,2,0:T(8,128)(2,1)S(1)} async-done(((bf16[16,128,224]{1,2,0:T(8,128)(2,1)}), bf16[16,128,224]{1,2,0:T(8,128)(2,1)S(1)}, u32[]{:S(2)}, u32[]{:S(2)}) %all-to-all-start) | async-done | bytes 917536 | tf_op jit(solution)/shard_map/all_to_all | solution.py:47
  307.5 151.2 %reduce-scatter.5.cloned.1.call-done = bf16[128,2048]{1,0:T(8,128)(2,1)} async-done(((bf16[2048,2048]{1,0:T(8,128)(2,1)}), bf16[128,2048]{1,0:T(8,128)(2,1)}) %reduce-scatter.5.cloned.1.call-update) | async-done | bytes 524304 | tf_op jit(solution)/shard_map/reduce_scatter | solution.py:53
  (65 shorter events, 27.9 us)
Async XLA Ops:
  7.2 114.8 %all-gather.4.cloned.1.call-start = ((), (), s32[]{:S(2)}) async-start(), calls=%async_computation.4 | async-start | bytes 8912896 | tf_op jit(solution)/shard_map/all_gather | solution.py:20
  7.9 168.2 %all-gather.6.cloned.1.call-start = ((), (), s32[]{:S(2)}) async-start(), calls=%async_computation.7 | async-start | bytes 25165824 | tf_op jit(solution)/shard_map/all_gather | solution.py:21
  122.0 1.2 copy-start
  123.1 7.6 %copy-start.5 = (f32[224,16]{0,1:T(8,128)S(1)}, f32[224,16]{0,1:T(8,128)}, u32[]{:S(2)}) copy-start(f32[224,16]{0,1:T(8,128)} %param.8) | copy-start | bytes 43012
  123.1 7.6 %copy-start.6 = (f32[224,16]{0,1:T(8,128)S(1)}, f32[224,16]{0,1:T(8,128)}, u32[]{:S(2)}) copy-start(f32[224,16]{0,1:T(8,128)} %param.10) | copy-start | bytes 43012
  124.4 70.0 %all-to-all-start.1 = ((bf16[128,16,224]{0,2,1:T(8,128)(2,1)}), bf16[128,16,224]{0,2,1:T(8,128)(2,1)S(1)}, u32[]{:S(2)}, u32[]{:S(2)}) async-start(bf16[128,16,224]{0,2,1:T(8,128)(2,1)} %bitcast.36), calls=%async_computation.1 | async-start | bytes 1835008 | tf_op jit(solution)/shard_map/all_to_all | solution.py:23
  130.7 132.2 %reduce-scatter.3.cloned.1.call-start = ((), (), s32[]{:S(2)}) async-start(), calls=%async_computation.5 | async-start | bytes 25165824 | tf_op jit(solution)/shard_map/reduce_scatter | solution.py:50
  139.2 1.0 copy-start.8
  154.6 14.8 %copy-start.9 = (bf16[224,2048]{1,0:T(8,128)(2,1)}, bf16[224,2048]{1,0:T(8,128)(2,1)S(1)}, u32[]{:S(2)}) copy-start(bf16[224,2048]{1,0:T(8,128)(2,1)S(1)} %get-tuple-element.60) | copy-start | bytes 2752516
  163.4 0.9 copy-start.7
  176.1 14.4 %copy-start.11 = (bf16[4096,2048]{1,0:T(8,128)(2,1)S(1)}, bf16[4096,2048]{1,0:T(8,128)(2,1)}, u32[]{:S(2)}) copy-start(bf16[4096,2048]{1,0:T(8,128)(2,1)} %all-gather.6.cloned.1.call-done) | copy-start | bytes 50331652
  183.8 6.7 %copy-start.10 = (bf16[224,2048]{1,0:T(8,128)(2,1)S(1)}, bf16[224,2048]{1,0:T(8,128)(2,1)}, u32[]{:S(2)}) copy-start(bf16[224,2048]{1,0:T(8,128)(2,1)} %copy-done.9) | copy-start | bytes 2752516
  194.4 0.9 copy-start.1
  204.6 15.0 %copy-start.3 = (bf16[2048,224]{0,1:T(8,128)(2,1)}, bf16[2048,224]{0,1:T(8,128)(2,1)S(1)}, u32[]{:S(2)}) copy-start(bf16[2048,224]{0,1:T(8,128)(2,1)S(1)} %get-tuple-element.8) | copy-start | bytes 2752516
  236.5 222.2 %reduce-scatter.5.cloned.1.call-start = ((), (), s32[]{:S(2)}) async-start(), calls=%async_computation.6 | async-start | bytes 8912896 | tf_op jit(solution)/shard_map/reduce_scatter | solution.py:53
  262.9 1.2 copy-start.2
  264.0 8.0 %copy-start.4 = (bf16[2048,224]{0,1:T(8,128)(2,1)S(1)}, bf16[2048,224]{0,1:T(8,128)(2,1)}, u32[]{:S(2)}) copy-start(bf16[2048,224]{0,1:T(8,128)(2,1)} %copy-done.3) | copy-start | bytes 2752516
  265.1 41.1 %all-to-all-start = ((bf16[16,128,224]{1,2,0:T(8,128)(2,1)}), bf16[16,128,224]{1,2,0:T(8,128)(2,1)S(1)}, u32[]{:S(2)}, u32[]{:S(2)}) async-start(bf16[16,128,224]{1,2,0:T(8,128)(2,1)} %bitcast.73), calls=%async_computation | async-start | bytes 1835008 | tf_op jit(solution)/shard_map/all_to_all | solution.py:47
  272.1 11.5 %slice-start = ((s8[16777216]{0:T(1024)(128)(4,1)}), s8[4194304]{0:T(1024)(128)(4,1)S(1)}, s32[]{:S(2)}) async-start(s8[16777216]{0:T(1024)(128)(4,1)} %bitcast.107), calls=%async_computation.8 | async-start | bytes 8388608
  272.1 11.5 %slice-start.1 = ((s8[16777216]{0:T(1024)(128)(4,1)}), s8[4194304]{0:T(1024)(128)(4,1)S(1)}, s32[]{:S(2)}) async-start(s8[16777216]{0:T(1024)(128)(4,1)} %bitcast.107), calls=%async_computation.9 | async-start | bytes 8388608
  277.9 5.6 %slice-start.2 = ((s8[16777216]{0:T(1024)(128)(4,1)}), s8[4194304]{0:T(1024)(128)(4,1)S(1)}, s32[]{:S(2)}) async-start(s8[16777216]{0:T(1024)(128)(4,1)} %bitcast.107), calls=%async_computation.10 | async-start | bytes 8388608
  278.0 5.8 %slice-start.3 = ((s8[16777216]{0:T(1024)(128)(4,1)}), s8[4194304]{0:T(1024)(128)(4,1)S(1)}, s32[]{:S(2)}) async-start(s8[16777216]{0:T(1024)(128)(4,1)} %bitcast.107), calls=%async_computation.11 | async-start | bytes 8388608
Sparse Core Ops, SparseCore 0:
  10.7 111.1 all-gather.3
  123.5 30.5 all-gather.5
  236.6 26.1 reduce-scatter.2
  265.6 193.1 reduce-scatter.4
where the time goes:
time: 467 us; the launch traced here: 465 us
  waiting for transfers between devices  307 us (66%)
  matrix products  75.2 us (16%)
  other arithmetic  46.8 us (10%)
  between operations  14.1 us (3%)
  starting transfers between devices  13.3 us (3%)
  local copies, waits for them, and re-layouts  8.98 us (2%)
    reduce_scatter x1, waiting for transfers between devices, per_device(): lax.psum_scatter(partial_sum, 'inter', scatter_dimension=0, tiled=True)  151 us
    all_gather x1, waiting for transfers between devices, per_device(): mine = lax.all_gather(tokens, 'inter', axis=0, tiled=True)  114 us
    unnamed x31, other arithmetic  40.6 us
    dot_general x4, matrix products, forward(): lax.dot_general(whole[s], weights[:, s * wide:(s + 1) * wide], (((1,), (1...  27.5 us
    reduce_scatter x1, waiting for transfers between devices, per_device(): lax.psum_scatter(partial_sum.astype(jnp.bfloat16), 'intra', scatter_dimen...  26.3 us
    dot_general x1, matrix products, per_device(): jnp.dot(d_up, w_up, preferred_element_type=jnp.float32)  16.9 us
    dot_general x4, matrix products, rows_grad(): lax.dot_general(d_rows, whole[s], (((0,), (0,)), ((), ())), preferred_ele...  15.7 us
    dot_general x1, matrix products, per_device(): partial_sum = jnp.dot(d_gate, w_gate, preferred_element_type=jnp.float32)  15 us
  transfers between devices with their start and end apart: 6, of which 4 were waited for; matrix products, arithmetic and copies ran while one was open for 18% of the time, Pallas kernels for 0%

commit v1 on v0

--- a/solution.py
+++ b/solution.py
@@ -17,7 +17,24 @@
 
 def per_device(tokens, gate_codes, gate_scales, up_codes, up_scales, cotangent):
     groups = lax.axis_size("inter")
-    mine = lax.all_gather(tokens, "inter", axis=0, tiled=True)
+    size, mine_2, rows_2 = (lax.axis_size("inter"), lax.axis_index("inter"), tokens.shape[0])
+    forward_2 = [(i, (i + 1) % size) for i in range(size)]
+    left = [(i, (i - 1) % size) for i in range(size)]
+    out = jnp.zeros((*tokens.shape[:0], size * rows_2, *tokens.shape[0 + 1 :]), tokens.dtype)
+    out = lax.dynamic_update_slice_in_dim(out, tokens, mine_2 * rows_2, axis=0)
+    from_left = from_right = tokens
+    middle = size // 2
+    for step_2 in range(1, middle + 1):
+        from_left = lax.ppermute(from_left, "inter", forward_2)
+        out = lax.dynamic_update_slice_in_dim(
+            out, from_left, (mine_2 - step_2) % size * rows_2, axis=0
+        )
+        if step_2 < size - middle:
+            from_right = lax.ppermute(from_right, "inter", left)
+            out = lax.dynamic_update_slice_in_dim(
+                out, from_right, (mine_2 + step_2) % size * rows_2, axis=0
+            )
+    mine = out
     whole = lax.all_gather(mine, "intra", axis=0, tiled=False)
     slabs, count, wide = whole.shape
     back = lax.all_to_all(cotangent, "inter", split_axis=1, concat_axis=0, tiled=True)

time: 467 us -> 546 us (1.17)
  waiting for transfers between devices: 307 us -> 348 us
  starting transfers between devices: 13.3 us -> 34.2 us
  local copies, waits for them, and re-layouts: 8.98 us -> 28.9 us
    ppermute x0 -> x15, waiting for transfers between devices: none -> 158 us  [the longest x8 96 us: per_device(): from_left = lax.ppermute(from_left, 'inter', forward_2)]
    all_gather x1 -> x0, waiting for transfers between devices: 114 us -> none  [per_device(): mine = lax.all_gather(tokens, 'inter', axis=0, tiled=True)]
    dynamic_update_slice x0 -> x16, local copies, waits for them, and re-layouts: none -> 13.5 us  [the longest x8 6.7 us: per_device(): lax.dynamic_update_slice_in_dim(out, from_left, (mine_2 - step_2) % size...]
    all_to_all x1, starting transfers between devices: 6.25 us -> 17.4 us  [per_device(): lax.all_to_all(cotangent, 'inter', split_axis=1, concat_axis=0, tiled=True)]
    ppermute x0 -> x15, starting transfers between devices: none -> 9.52 us  [the longest x8 8.92 us: per_device(): from_left = lax.ppermute(from_left, 'inter', forward_2)]
  transfers between devices with their start and end apart: 6 -> 20, of which waited for: 4 -> 17; matrix products, arithmetic and copies ran while one was open for 18% -> 17% of each run, Pallas kernels for 0% -> 0%
where the time goes in v1:
time: 546 us; the launch traced here: 544 us
  waiting for transfers between devices  348 us (64%)
  matrix products  72.7 us (13%)
  other arithmetic  46.7 us (9%)
  starting transfers between devices  34.2 us (6%)
  local copies, waits for them, and re-layouts  28.9 us (5%)
  between operations  14.1 us (3%)
    reduce_scatter x1, waiting for transfers between devices, per_device(): lax.psum_scatter(partial_sum, 'inter', scatter_dimension=0, tiled=True)  149 us
    ppermute x8, waiting for transfers between devices, per_device(): from_left = lax.ppermute(from_left, 'inter', forward_2)  96 us
    ppermute x7, waiting for transfers between devices, per_device(): from_right = lax.ppermute(from_right, 'inter', left)  61.8 us
    unnamed x31, other arithmetic  40.4 us
    reduce_scatter x1, waiting for transfers between devices, per_device(): lax.psum_scatter(partial_sum.astype(jnp.bfloat16), 'intra', scatter_dimen...  26.3 us
    dot_general x4, matrix products, forward(): lax.dot_general(whole[s], weights[:, s * wide:(s + 1) * wide], (((1,), (1...  24.9 us
    all_to_all x1, starting transfers between devices, per_device(): lax.all_to_all(cotangent, 'inter', split_axis=1, concat_axis=0, tiled=True)  17.4 us
    dot_general x1, matrix products, per_device(): jnp.dot(d_up, w_up, preferred_element_type=jnp.float32)  16.9 us
  transfers between devices with their start and end apart: 20, of which 17 were waited for; matrix products, arithmetic and copies ran while one was open for 17% of the time, Pallas kernels for 0%

profile of v1, /device:TPU:26, one launch (start us, length us, event | category | flops | bytes accessed | tf_op | source)
XLA Modules:
  0.0 544.5 jit_solution(3375337935402846439)
XLA Ops:
  7.8 2.4 collective-permute-start
  10.2 4.4 all_gather.38
  15.5 7.7 %collective-permute-done.1 = bf16[128,2048]{1,0:T(8,128)(2,1)S(1)} collective-permute-done((bf16[128,2048]{1,0:T(8,128)(2,1)}, bf16[128,2048]{1,0:T(8,128)(2,1)S(1)}, u32[]{:S(2)}, u32[]{:S(2)}) %collective-permute-start.1) | collective-permute-done | bytes 524320 | tf_op jit(solution)/shard_map/ppermute | solution.py:33
  23.2 10.1 %collective-permute-done = bf16[128,2048]{1,0:T(8,128)(2,1)S(1)} collective-permute-done((bf16[128,2048]{1,0:T(8,128)(2,1)}, bf16[128,2048]{1,0:T(8,128)(2,1)S(1)}, u32[]{:S(2)}, u32[]{:S(2)}) %collective-permute-start) | collective-permute-done | bytes 524320 | tf_op jit(solution)/shard_map/ppermute | solution.py:28
  36.6 10.0 %collective-permute-done.3 = bf16[128,2048]{1,0:T(8,128)(2,1)S(1)} collective-permute-done((bf16[128,2048]{1,0:T(8,128)(2,1)S(1)}, bf16[128,2048]{1,0:T(8,128)(2,1)S(1)}, u32[]{:S(2)}, u32[]{:S(2)}) %collective-permute-start.3) | collective-permute-done | bytes 524320 | tf_op jit(solution)/shard_map/ppermute | solution.py:33
  46.6 10.7 %collective-permute-done.2 = bf16[128,2048]{1,0:T(8,128)(2,1)S(1)} collective-permute-done((bf16[128,2048]{1,0:T(8,128)(2,1)S(1)}, bf16[128,2048]{1,0:T(8,128)(2,1)S(1)}, u32[]{:S(2)}, u32[]{:S(2)}) %collective-permute-start.2) | collective-permute-done | bytes 524320 | tf_op jit(solution)/shard_map/ppermute | solution.py:28
  59.6 11.1 %collective-permute-done.5 = bf16[128,2048]{1,0:T(8,128)(2,1)S(1)} collective-permute-done((bf16[128,2048]{1,0:T(8,128)(2,1)S(1)}, bf16[128,2048]{1,0:T(8,128)(2,1)S(1)}, u32[]{:S(2)}, u32[]{:S(2)}) %collective-permute-start.5) | collective-permute-done | bytes 524320 | tf_op jit(solution)/shard_map/ppermute | solution.py:33
  70.7 10.8 %collective-permute-done.4 = bf16[128,2048]{1,0:T(8,128)(2,1)S(1)} collective-permute-done((bf16[128,2048]{1,0:T(8,128)(2,1)S(1)}, bf16[128,2048]{1,0:T(8,128)(2,1)S(1)}, u32[]{:S(2)}, u32[]{:S(2)}) %collective-permute-start.4) | collective-permute-done | bytes 524320 | tf_op jit(solution)/shard_map/ppermute | solution.py:28
  83.6 11.1 %collective-permute-done.7 = bf16[128,2048]{1,0:T(8,128)(2,1)S(1)} collective-permute-done((bf16[128,2048]{1,0:T(8,128)(2,1)S(1)}, bf16[128,2048]{1,0:T(8,128)(2,1)S(1)}, u32[]{:S(2)}, u32[]{:S(2)}) %collective-permute-start.7) | collective-permute-done | bytes 524320 | tf_op jit(solution)/shard_map/ppermute | solution.py:33
  94.7 11.1 %collective-permute-done.6 = bf16[128,2048]{1,0:T(8,128)(2,1)S(1)} collective-permute-done((bf16[128,2048]{1,0:T(8,128)(2,1)S(1)}, bf16[128,2048]{1,0:T(8,128)(2,1)S(1)}, u32[]{:S(2)}, u32[]{:S(2)}) %collective-permute-start.6) | collective-permute-done | bytes 524320 | tf_op jit(solution)/shard_map/ppermute | solution.py:28
  107.7 11.1 %collective-permute-done.9 = bf16[128,2048]{1,0:T(8,128)(2,1)S(1)} collective-permute-done((bf16[128,2048]{1,0:T(8,128)(2,1)S(1)}, bf16[128,2048]{1,0:T(8,128)(2,1)S(1)}, u32[]{:S(2)}, u32[]{:S(2)}) %collective-permute-start.9) | collective-permute-done | bytes 524320 | tf_op jit(solution)/shard_map/ppermute | solution.py:33
  118.8 11.4 %collective-permute-done.8 = bf16[128,2048]{1,0:T(8,128)(2,1)S(1)} collective-permute-done((bf16[128,2048]{1,0:T(8,128)(2,1)S(1)}, bf16[128,2048]{1,0:T(8,128)(2,1)S(1)}, u32[]{:S(2)}, u32[]{:S(2)}) %collective-permute-start.8) | collective-permute-done | bytes 524320 | tf_op jit(solution)/shard_map/ppermute | solution.py:28
  132.0 10.8 %collective-permute-done.11 = bf16[128,2048]{1,0:T(8,128)(2,1)S(1)} collective-permute-done((bf16[128,2048]{1,0:T(8,128)(2,1)S(1)}, bf16[128,2048]{1,0:T(8,128)(2,1)S(1)}, u32[]{:S(2)}, u32[]{:S(2)}) %collective-permute-start.11) | collective-permute-done | bytes 524320 | tf_op jit(solution)/shard_map/ppermute | solution.py:33
  142.8 16.4 %collective-permute-done.10 = bf16[128,2048]{1,0:T(8,128)(2,1)S(1)} collective-permute-done((bf16[128,2048]{1,0:T(8,128)(2,1)S(1)}, bf16[128,2048]{1,0:T(8,128)(2,1)S(1)}, u32[]{:S(2)}, u32[]{:S(2)}) %collective-permute-start.10) | collective-permute-done | bytes 524320 | tf_op jit(solution)/shard_map/ppermute | solution.py:28
  160.9 17.8 %collective-permute-done.12 = bf16[128,2048]{1,0:T(8,128)(2,1)S(1)} collective-permute-done((bf16[128,2048]{1,0:T(8,128)(2,1)S(1)}, bf16[128,2048]{1,0:T(8,128)(2,1)S(1)}, u32[]{:S(2)}, u32[]{:S(2)}) %collective-permute-start.12) | collective-permute-done | bytes 524320 | tf_op jit(solution)/shard_map/ppermute | solution.py:28
  178.7 3.5 collective-permute-start.14
  183.8 7.8 %collective-permute-done.14 = bf16[128,2048]{1,0:T(8,128)(2,1)S(1)} collective-permute-done((bf16[128,2048]{1,0:T(8,128)(2,1)S(1)}, bf16[128,2048]{1,0:T(8,128)(2,1)S(1)}, u32[]{:S(2)}, u32[]{:S(2)}) %collective-permute-start.14) | collective-permute-done | bytes 524320 | tf_op jit(solution)/shard_map/ppermute | solution.py:28
  194.9 17.4 %all-to-all-start.1 = ((bf16[128,16,224]{0,2,1:T(8,128)(2,1)}), bf16[128,16,224]{0,2,1:T(8,128)(2,1)S(1)}, u32[]{:S(2)}, u32[]{:S(2)}) async-start(bf16[128,16,224]{0,2,1:T(8,128)(2,1)} %bitcast.52), calls=%async_computation.1 | async-start | bytes 1835008 | tf_op jit(solution)/shard_map/all_to_all | solution.py:40
  257.8 6.4 %fusion.6 = f32[2048,224]{0,1:T(8,128)S(1)} fusion(bf16[224,2048]{1,0:T(8,128)(2,1)} %copy-done.8, bf16[2,2048,2048]{2,1,0:T(8,128)(2,1)} %all-gather.2.cloned.1.call-done), kind=kOutput, calls=%fused_computation.9 | convolution fusion | flops 1879048192 | bytes 11141120 | tf_op jit(solution)/shard_map/dot_general | solution.py:47
  266.2 5.2 fusion.7
  271.4 3.9 fusion.9
  276.2 9.5 %fusion.13 = (bf16[2048,224]{0,1:T(8,128)(2,1)S(1)}, bf16[2048,224]{0,1:T(8,128)(2,1)S(1)}, bf16[28,16,8,128]{3,2,1,0:T(8,128)(2,1)}) fusion(f32[2048,224]{0,1:T(8,128)} %fusion.9, f32[2048,224]{0,1:T(8,128)} %fusion.7, bf16[224,2048]{1,0:T(8,128)(2,1)} %copy-done.11, bf16[2,2048,2048]{2,1,0:T(8,128)(2,1)} %all-gather.2.cloned.1.call-done, ...), kind=kOutput, calls=%fused_computation.20 | convolution fusion | flops 1886846976 | bytes 16646144 | tf_op jit(solution)/shard_map/dot_general | solution.py:47
  285.7 15.0 %fusion.18 = f32[2048,4096]{1,0:T(8,128)} fusion(bf16[2048,224]{0,1:T(8,128)(2,1)S(1)} %get-tuple-element.13, bf16[224,4096]{1,0:T(8,128)(2,1)} %get-tuple-element.47), kind=kOutput, calls=%fused_computation.141 | convolution fusion | flops 3758096384 | bytes 36306944 | tf_op jit(solution)/shard_map/dot_general | solution.py:65
  300.7 16.9 %add_convert_fusion = bf16[2048,4096]{1,0:T(8,128)(2,1)} fusion(f32[2048,4096]{1,0:T(8,128)} %fusion.18, bf16[2048,224]{0,1:T(8,128)(2,1)S(1)} %get-tuple-element.12, bf16[224,4096]{1,0:T(8,128)(2,1)S(1)} %get-tuple-element.15), kind=kOutput, calls=%fused_computation | convolution fusion | flops 3774873600 | bytes 53084160 | tf_op jit(solution)/shard_map/dot_general | solution.py:66
  317.7 26.3 %reduce-scatter.3.cloned.1.call-done = bf16[2048,2048]{1,0:T(8,128)(2,1)} async-done(((bf16[2048,4096]{1,0:T(8,128)(2,1)}), bf16[2048,2048]{1,0:T(8,128)(2,1)}) %reduce-scatter.3.cloned.1.call-update) | async-done | bytes 8388624 | tf_op jit(solution)/shard_map/reduce_scatter | solution.py:67
  346.3 6.9 %all-to-all-start = ((bf16[16,128,224]{1,2,0:T(8,128)(2,1)}), bf16[16,128,224]{1,2,0:T(8,128)(2,1)S(1)}, u32[]{:S(2)}, u32[]{:S(2)}) async-start(bf16[16,128,224]{1,2,0:T(8,128)(2,1)} %bitcast.117), calls=%async_computation | async-start | bytes 1835008 | tf_op jit(solution)/shard_map/all_to_all | solution.py:64
  353.2 5.9 %fusion.4 = f32[224,2048]{1,0:T(8,128)S(1)} fusion(bf16[2048,224]{0,1:T(8,128)(2,1)S(1)} %copy-done.4, bf16[2,2048,2048]{2,1,0:T(8,128)(2,1)} %all-gather.2.cloned.1.call-done), kind=kOutput, calls=%fused_computation.7 | convolution fusion | flops 1879048192 | bytes 11141120 | tf_op jit(solution)/shard_map/dot_general | solution.py:74
  359.2 5.6 %fusion = f32[224,2048]{1,0:T(8,128)S(1)} fusion(bf16[2048,224]{0,1:T(8,128)(2,1)S(1)} %copy-done.4, bf16[2,2048,2048]{2,1,0:T(8,128)(2,1)} %all-gather.2.cloned.1.call-done), kind=kOutput, calls=%fused_computation.3 | convolution fusion | flops 1879048192 | bytes 11141120 | tf_op jit(solution)/shard_map/dot_general | solution.py:74
  367.1 2.1 fusion.1
  369.3 3.5 maximum_multiply_fusion
  372.8 14.6 %all-to-all-done = bf16[16,128,224]{1,2,0:T(8,128)(2,1)S(1)} async-done(((bf16[16,128,224]{1,2,0:T(8,128)(2,1)}), bf16[16,128,224]{1,2,0:T(8,128)(2,1)S(1)}, u32[]{:S(2)}, u32[]{:S(2)}) %all-to-all-start) | async-done | bytes 917536 | tf_op jit(solution)/shard_map/all_to_all | solution.py:64
  388.7 149.3 %reduce-scatter.5.cloned.1.call-done = bf16[128,2048]{1,0:T(8,128)(2,1)} async-done(((bf16[2048,2048]{1,0:T(8,128)(2,1)}), bf16[128,2048]{1,0:T(8,128)(2,1)}) %reduce-scatter.5.cloned.1.call-update) | async-done | bytes 524304 | tf_op jit(solution)/shard_map/reduce_scatter | solution.py:70
  (111 shorter events, 73.8 us)
Async XLA Ops:
  7.2 250.6 %all-gather.2.cloned.1.call-start = ((), (), s32[]{:S(2)}) async-start(), calls=%async_computation.4 | async-start | bytes 25165824 | tf_op jit(solution)/shard_map/all_gather | solution.py:38
  7.2 16.0 %collective-permute-start.1 = (bf16[128,2048]{1,0:T(8,128)(2,1)}, bf16[128,2048]{1,0:T(8,128)(2,1)S(1)}, u32[]{:S(2)}, u32[]{:S(2)}) collective-permute-start(bf16[128,2048]{1,0:T(8,128)(2,1)} %param.6), channel_id=1, source_target_pairs={{0,30},{2,0},{4,2},{6,4},{8,6},{10,8},{12,10},{14,12},{16,14},{18,... | collective-permute-start | bytes 1572872 | tf_op jit(solution)/shard_map/ppermute | solution.py:33
  7.8 25.5 %collective-permute-start = (bf16[128,2048]{1,0:T(8,128)(2,1)}, bf16[128,2048]{1,0:T(8,128)(2,1)S(1)}, u32[]{:S(2)}, u32[]{:S(2)}) collective-permute-start(bf16[128,2048]{1,0:T(8,128)(2,1)} %param.6), channel_id=1, source_target_pairs={{0,2},{2,4},{4,6},{6,8},{8,10},{10,12},{12,14},{14,16},{16,18},{18... | collective-permute-start | bytes 1572872 | tf_op jit(solution)/shard_map/ppermute | solution.py:28
  10.2 4.4 copy-start.5
  23.2 23.5 %collective-permute-start.3 = (bf16[128,2048]{1,0:T(8,128)(2,1)S(1)}, bf16[128,2048]{1,0:T(8,128)(2,1)S(1)}, u32[]{:S(2)}, u32[]{:S(2)}) collective-permute-start(bf16[128,2048]{1,0:T(8,128)(2,1)S(1)} %collective-permute-done.1), channel_id=1, source_target_pairs={{0,30},{2,0},{4,2},{6,4},{8,6},{10,8},{12,10},{14,12},{16,14},{18,... | collective-permute-start | bytes 1572872 | tf_op jit(solution)/shard_map/ppermute | solution.py:33
  33.2 24.0 %collective-permute-start.2 = (bf16[128,2048]{1,0:T(8,128)(2,1)S(1)}, bf16[128,2048]{1,0:T(8,128)(2,1)S(1)}, u32[]{:S(2)}, u32[]{:S(2)}) collective-permute-start(bf16[128,2048]{1,0:T(8,128)(2,1)S(1)} %collective-permute-done), channel_id=1, source_target_pairs={{0,2},{2,4},{4,6},{6,8},{8,10},{10,12},{12,14},{14,16},{16,18},{18... | collective-permute-start | bytes 1572872 | tf_op jit(solution)/shard_map/ppermute | solution.py:28
  46.6 24.0 %collective-permute-start.5 = (bf16[128,2048]{1,0:T(8,128)(2,1)S(1)}, bf16[128,2048]{1,0:T(8,128)(2,1)S(1)}, u32[]{:S(2)}, u32[]{:S(2)}) collective-permute-start(bf16[128,2048]{1,0:T(8,128)(2,1)S(1)} %collective-permute-done.3), channel_id=1, source_target_pairs={{0,30},{2,0},{4,2},{6,4},{8,6},{10,8},{12,10},{14,12},{16,14},{18,... | collective-permute-start | bytes 1572872 | tf_op jit(solution)/shard_map/ppermute | solution.py:33
  57.3 24.1 %collective-permute-start.4 = (bf16[128,2048]{1,0:T(8,128)(2,1)S(1)}, bf16[128,2048]{1,0:T(8,128)(2,1)S(1)}, u32[]{:S(2)}, u32[]{:S(2)}) collective-permute-start(bf16[128,2048]{1,0:T(8,128)(2,1)S(1)} %collective-permute-done.2), channel_id=1, source_target_pairs={{0,2},{2,4},{4,6},{6,8},{8,10},{10,12},{12,14},{14,16},{16,18},{18... | collective-permute-start | bytes 1572872 | tf_op jit(solution)/shard_map/ppermute | solution.py:28
  70.7 24.0 %collective-permute-start.7 = (bf16[128,2048]{1,0:T(8,128)(2,1)S(1)}, bf16[128,2048]{1,0:T(8,128)(2,1)S(1)}, u32[]{:S(2)}, u32[]{:S(2)}) collective-permute-start(bf16[128,2048]{1,0:T(8,128)(2,1)S(1)} %collective-permute-done.5), channel_id=1, source_target_pairs={{0,30},{2,0},{4,2},{6,4},{8,6},{10,8},{12,10},{14,12},{16,14},{18,... | collective-permute-start | bytes 1572872 | tf_op jit(solution)/shard_map/ppermute | solution.py:33
  81.4 24.4 %collective-permute-start.6 = (bf16[128,2048]{1,0:T(8,128)(2,1)S(1)}, bf16[128,2048]{1,0:T(8,128)(2,1)S(1)}, u32[]{:S(2)}, u32[]{:S(2)}) collective-permute-start(bf16[128,2048]{1,0:T(8,128)(2,1)S(1)} %collective-permute-done.4), channel_id=1, source_target_pairs={{0,2},{2,4},{4,6},{6,8},{8,10},{10,12},{12,14},{14,16},{16,18},{18... | collective-permute-start | bytes 1572872 | tf_op jit(solution)/shard_map/ppermute | solution.py:28
  94.7 24.1 %collective-permute-start.9 = (bf16[128,2048]{1,0:T(8,128)(2,1)S(1)}, bf16[128,2048]{1,0:T(8,128)(2,1)S(1)}, u32[]{:S(2)}, u32[]{:S(2)}) collective-permute-start(bf16[128,2048]{1,0:T(8,128)(2,1)S(1)} %collective-permute-done.7), channel_id=1, source_target_pairs={{0,30},{2,0},{4,2},{6,4},{8,6},{10,8},{12,10},{14,12},{16,14},{18,... | collective-permute-start | bytes 1572872 | tf_op jit(solution)/shard_map/ppermute | solution.py:33
  105.8 24.4 %collective-permute-start.8 = (bf16[128,2048]{1,0:T(8,128)(2,1)S(1)}, bf16[128,2048]{1,0:T(8,128)(2,1)S(1)}, u32[]{:S(2)}, u32[]{:S(2)}) collective-permute-start(bf16[128,2048]{1,0:T(8,128)(2,1)S(1)} %collective-permute-done.6), channel_id=1, source_target_pairs={{0,2},{2,4},{4,6},{6,8},{8,10},{10,12},{12,14},{14,16},{16,18},{18... | collective-permute-start | bytes 1572872 | tf_op jit(solution)/shard_map/ppermute | solution.py:28
  118.8 24.0 %collective-permute-start.11 = (bf16[128,2048]{1,0:T(8,128)(2,1)S(1)}, bf16[128,2048]{1,0:T(8,128)(2,1)S(1)}, u32[]{:S(2)}, u32[]{:S(2)}) collective-permute-start(bf16[128,2048]{1,0:T(8,128)(2,1)S(1)} %collective-permute-done.9), channel_id=1, source_target_pairs={{0,30},{2,0},{4,2},{6,4},{8,6},{10,8},{12,10},{14,12},{16,14},{18,... | collective-permute-start | bytes 1572872 | tf_op jit(solution)/shard_map/ppermute | solution.py:33
  130.2 28.9 %collective-permute-start.10 = (bf16[128,2048]{1,0:T(8,128)(2,1)S(1)}, bf16[128,2048]{1,0:T(8,128)(2,1)S(1)}, u32[]{:S(2)}, u32[]{:S(2)}) collective-permute-start(bf16[128,2048]{1,0:T(8,128)(2,1)S(1)} %collective-permute-done.8), channel_id=1, source_target_pairs={{0,2},{2,4},{4,6},{6,8},{8,10},{10,12},{12,14},{14,16},{16,18},{18... | collective-permute-start | bytes 1572872 | tf_op jit(solution)/shard_map/ppermute | solution.py:28
  142.8 40.2 %collective-permute-start.13 = (bf16[128,2048]{1,0:T(8,128)(2,1)S(1)}, bf16[128,2048]{1,0:T(8,128)(2,1)S(1)}, u32[]{:S(2)}, u32[]{:S(2)}) collective-permute-start(bf16[128,2048]{1,0:T(8,128)(2,1)S(1)} %collective-permute-done.11), channel_id=1, source_target_pairs={{0,30},{2,0},{4,2},{6,4},{8,6},{10,8},{12,10},{14,12},{16,14},{18,... | collective-permute-start | bytes 1572872 | tf_op jit(solution)/shard_map/ppermute | solution.py:33
  159.2 19.5 %collective-permute-start.12 = (bf16[128,2048]{1,0:T(8,128)(2,1)S(1)}, bf16[128,2048]{1,0:T(8,128)(2,1)S(1)}, u32[]{:S(2)}, u32[]{:S(2)}) collective-permute-start(bf16[128,2048]{1,0:T(8,128)(2,1)S(1)} %collective-permute-done.10), channel_id=1, source_target_pairs={{0,2},{2,4},{4,6},{6,8},{8,10},{10,12},{12,14},{14,16},{16,18},{18... | collective-permute-start | bytes 1572872 | tf_op jit(solution)/shard_map/ppermute | solution.py:28
  178.7 13.0 %collective-permute-start.14 = (bf16[128,2048]{1,0:T(8,128)(2,1)S(1)}, bf16[128,2048]{1,0:T(8,128)(2,1)S(1)}, u32[]{:S(2)}, u32[]{:S(2)}) collective-permute-start(bf16[128,2048]{1,0:T(8,128)(2,1)S(1)} %collective-permute-done.12), channel_id=1, source_target_pairs={{0,2},{2,4},{4,6},{6,8},{8,10},{10,12},{12,14},{14,16},{16,18},{18... | collective-permute-start | bytes 1572872 | tf_op jit(solution)/shard_map/ppermute | solution.py:28
  193.7 18.9 %copy-start.6 = (f32[224,16]{0,1:T(8,128)S(1)}, f32[224,16]{0,1:T(8,128)}, u32[]{:S(2)}) copy-start(f32[224,16]{0,1:T(8,128)} %param.8) | copy-start | bytes 43012
  193.7 19.0 %copy-start.7 = (f32[224,16]{0,1:T(8,128)S(1)}, f32[224,16]{0,1:T(8,128)}, u32[]{:S(2)}) copy-start(f32[224,16]{0,1:T(8,128)} %param.10) | copy-start | bytes 43012
  194.9 80.3 %all-to-all-start.1 = ((bf16[128,16,224]{0,2,1:T(8,128)(2,1)}), bf16[128,16,224]{0,2,1:T(8,128)(2,1)S(1)}, u32[]{:S(2)}, u32[]{:S(2)}) async-start(bf16[128,16,224]{0,2,1:T(8,128)(2,1)} %bitcast.52), calls=%async_computation.1 | async-start | bytes 1835008 | tf_op jit(solution)/shard_map/all_to_all | solution.py:40
  212.4 131.7 %reduce-scatter.3.cloned.1.call-start = ((), (), s32[]{:S(2)}) async-start(), calls=%async_computation.5 | async-start | bytes 25165824 | tf_op jit(solution)/shard_map/reduce_scatter | solution.py:67
  236.2 14.8 %copy-start.11 = (bf16[224,2048]{1,0:T(8,128)(2,1)}, bf16[224,2048]{1,0:T(8,128)(2,1)S(1)}, u32[]{:S(2)}) copy-start(bf16[224,2048]{1,0:T(8,128)(2,1)S(1)} %get-tuple-element.64) | copy-start | bytes 2752516
  257.8 8.4 %copy-start.12 = (bf16[2,2048,2048]{2,1,0:T(8,128)(2,1)S(1)}, bf16[2,2048,2048]{2,1,0:T(8,128)(2,1)}, u32[]{:S(2)}) copy-start(bf16[2,2048,2048]{2,1,0:T(8,128)(2,1)} %all-gather.2.cloned.1.call-done) | copy-start | bytes 50331652
  266.2 5.2 copy-start.10
  285.7 15.0 %copy-start.3 = (bf16[2048,224]{0,1:T(8,128)(2,1)}, bf16[2048,224]{0,1:T(8,128)(2,1)S(1)}, u32[]{:S(2)}) copy-start(bf16[2048,224]{0,1:T(8,128)(2,1)S(1)} %get-tuple-element.12) | copy-start | bytes 2752516
  317.7 220.3 %reduce-scatter.5.cloned.1.call-start = ((), (), s32[]{:S(2)}) async-start(), calls=%async_computation.6 | async-start | bytes 8912896 | tf_op jit(solution)/shard_map/reduce_scatter | solution.py:70
  345.2 8.0 %copy-start.4 = (bf16[2048,224]{0,1:T(8,128)(2,1)S(1)}, bf16[2048,224]{0,1:T(8,128)(2,1)}, u32[]{:S(2)}) copy-start(bf16[2048,224]{0,1:T(8,128)(2,1)} %copy-done.3) | copy-start | bytes 2752516
  346.3 41.1 %all-to-all-start = ((bf16[16,128,224]{1,2,0:T(8,128)(2,1)}), bf16[16,128,224]{1,2,0:T(8,128)(2,1)S(1)}, u32[]{:S(2)}, u32[]{:S(2)}) async-start(bf16[16,128,224]{1,2,0:T(8,128)(2,1)} %bitcast.117), calls=%async_computation | async-start | bytes 1835008 | tf_op jit(solution)/shard_map/all_to_all | solution.py:64
  353.2 11.6 %slice-start = ((s8[16777216]{0:T(1024)(128)(4,1)}), s8[4194304]{0:T(1024)(128)(4,1)S(1)}, s32[]{:S(2)}) async-start(s8[16777216]{0:T(1024)(128)(4,1)} %bitcast.151), calls=%async_computation.7 | async-start | bytes 8388608
  353.2 11.6 %slice-start.1 = ((s8[16777216]{0:T(1024)(128)(4,1)}), s8[4194304]{0:T(1024)(128)(4,1)S(1)}, s32[]{:S(2)}) async-start(s8[16777216]{0:T(1024)(128)(4,1)} %bitcast.151), calls=%async_computation.8 | async-start | bytes 8388608
  359.2 5.6 %slice-start.2 = ((s8[16777216]{0:T(1024)(128)(4,1)}), s8[4194304]{0:T(1024)(128)(4,1)S(1)}, s32[]{:S(2)}) async-start(s8[16777216]{0:T(1024)(128)(4,1)} %bitcast.151), calls=%async_computation.9 | async-start | bytes 8388608
  359.2 5.8 %slice-start.3 = ((s8[16777216]{0:T(1024)(128)(4,1)}), s8[4194304]{0:T(1024)(128)(4,1)S(1)}, s32[]{:S(2)}) async-start(s8[16777216]{0:T(1024)(128)(4,1)} %bitcast.151), calls=%async_computation.10 | async-start | bytes 8388608
  (5 other events, 5.1 us)
Sparse Core Ops, SparseCore 0:
  192.6 39.5 all-gather.1
  317.8 26.1 reduce-scatter.2
  346.9 191.0 reduce-scatter.4
